TPU v7x, 256 devices: a whole 4x4x8 slice. The times are simulated.
256 devices in a mesh: row: 8 (over z), col: 32 (over y, x, core).
Axes of the slice: x: 4, y: 4, z: 8, core: 2. Of those that a mesh axis runs over, the one named last changes fastest.
Arguments:
- sources: float32 [30, 32768], P(None, ('row', 'col')), may hold values from -12 to 12
- log_source_mass: float32 [32768], P(('row', 'col')), may hold values from -4 to 4
- targets: float32 [30, 16384], P(None, 'col'), may hold values from -6 to 6
- log_target_mass: float32 [16384], P('col'), may hold values from -4 to 4
- start_potential: float32 [16384], P('col'), may hold values from -12 to 250
Outputs:
- row_potential: float32 [32768], P(('row', 'col'))
- column_potential: float32 [16384], P('col')
All inputs are finite; a program needn't handle non-finite values.
Results may differ from a plain program's by a relative error of at most 0.00015.
Values sent between devices are 32-bit elements; how exact they have to be, the bound alone decides.
No kernel may reach another device: no remote copies, remote signals or barrier semaphores. Data moves between devices by JAX's collectives and lax.ppermute only.
A program may use at most 64 MiB of HBM per device.

v0:
```python
import math
import jax
import jax.numpy as jnp
from jax import lax
from jax.sharding import PartitionSpec as P

ITERS = 2
entropic_scale = 2.0
lowest = -1e30
block_width = 2048


def merged(shard, axis, combine):
    everything = jax.tree.map(lambda part: lax.all_gather(part, axis), shard)
    leading = jax.tree.map(lambda part: part[0], everything)

    def lap(k, so_far):
        return combine(so_far, jax.tree.map(lambda part: part[k], everything))

    return lax.fori_loop(1, lax.axis_size(axis), lap, leading)


def tile_scores(own_coords, own_sq, other):
    dims = own_coords.shape[0]
    coords = other[:dims]
    inner = lax.dot_general(
        own_coords,
        coords,
        (((0,), (0,)), ((), ())),
        precision=lax.Precision.HIGHEST,
        preferred_element_type=jnp.float32,
    )
    other_sq = 0.5 * jnp.sum(coords * coords, axis=0)
    cost = own_sq[:, None] + other_sq[None, :] - inner
    return other[dims][None, :] - cost / entropic_scale


def merge_pair(first, second):
    peak = jnp.maximum(first[0], second[0])
    return (peak, first[1] * jnp.exp(first[0] - peak) + second[1] * jnp.exp(second[0] - peak))


def online_fold(own_coords, partial_value, piece):
    own_sq = 0.5 * jnp.sum(own_coords * own_coords, axis=0)
    length = piece.shape[1]
    width = math.gcd(length, block_width)
    blocks = piece.reshape(piece.shape[0], length // width, width).transpose(1, 0, 2)

    def advance(running, block):
        scores = tile_scores(own_coords, own_sq, block)
        block_max = jnp.max(scores, axis=1)
        block_sum = jnp.sum(jnp.exp(scores - block_max[:, None]), axis=1)
        return (merge_pair(running, (block_max, block_sum)), None)

    result, unused = lax.scan(advance, partial_value, blocks)
    return result


def column_partials(row_block, all_columns):
    dims = row_block.shape[0] - 1
    coords = all_columns[:dims]
    count = coords.shape[1]
    width = math.gcd(count, block_width)
    blocks = coords.reshape(dims, count // width, width).transpose(1, 0, 2)
    row_sq = 0.5 * jnp.sum(row_block[:dims] * row_block[:dims], axis=0)

    def one_block(block):
        inner = lax.dot_general(
            row_block[:dims],
            block,
            (((0,), (0,)), ((), ())),
            precision=lax.Precision.HIGHEST,
            preferred_element_type=jnp.float32,
        )
        cost = row_sq[:, None] + 0.5 * jnp.sum(block * block, axis=0)[None, :] - inner
        scores = row_block[dims][:, None] - cost / entropic_scale
        block_max = jnp.max(scores, axis=0)
        return (block_max, jnp.sum(jnp.exp(scores - block_max[None, :]), axis=0))

    peaks, totals = lax.map(one_block, blocks)
    return (peaks.reshape(count), totals.reshape(count))


def on_device(sources, log_source_mass, targets, log_target_mass, start_potential):
    own_rows = sources.shape[1]
    own_cols = targets.shape[1]
    target_term = start_potential / entropic_scale + log_target_mass
    row_potential = jnp.zeros((own_rows,), jnp.float32)
    column_potential = start_potential
    for sweep in range(ITERS):
        target_pack = jnp.concatenate([targets, target_term[None, :]], axis=0)
        row_start = (
            jnp.full((own_rows,), lowest, jnp.float32),
            jnp.zeros((own_rows,), jnp.float32),
        )
        gathered = lax.all_gather(target_pack, "col", axis=1, tiled=True)
        row_peak, row_total = online_fold(sources, row_start, gathered)
        row_potential = -entropic_scale * (row_peak + jnp.log(row_total))
        source_term = row_potential / entropic_scale + log_source_mass
        source_pack = jnp.concatenate([sources, source_term[None, :]], axis=0)
        wide_peak, wide_total = column_partials(source_pack, gathered)
        blocks_count = lax.axis_size("col")
        peak_rows, total_rows = (
            lax.all_to_all(
                wide_peak.reshape(blocks_count, own_cols),
                "col",
                split_axis=0,
                concat_axis=0,
                tiled=True,
            ),
            lax.all_to_all(
                wide_total.reshape(blocks_count, own_cols),
                "col",
                split_axis=0,
                concat_axis=0,
                tiled=True,
            ),
        )
        local_peak = jnp.max(peak_rows, axis=0)
        local_total = jnp.sum(total_rows * jnp.exp(peak_rows - local_peak[None, :]), axis=0)
        col_peak, col_total = merged((local_peak, local_total), "row", merge_pair)
        column_potential = -entropic_scale * (col_peak + jnp.log(col_total))
        target_term = column_potential / entropic_scale + log_target_mass
    return (row_potential, column_potential)


def solution(mesh):
    return jax.shard_map(
        on_device,
        mesh=mesh,
        in_specs=(P(None, ("row", "col")), P(("row", "col")), P(None, "col"), P("col"), P("col")),
        out_specs=(P(("row", "col")), P("col")),
        check_vma=False,
    )
```

profile of v0, /device:TPU:2, one launch (start us, length us, event | category | flops | bytes accessed | tf_op | source)
XLA Modules:
  0.0 385.1 jit_solution(970008191891067864)
XLA Ops:
  10.2 51.7 %all-gather.11.cloned.1.call-done = f32[31,16384]{1,0:T(8,128)} async-done(((f32[31,512]{1,0:T(8,128)}), f32[31,16384]{1,0:T(8,128)}) %all-gather.11.cloned.1.call-update) | async-done | bytes 2031632 | tf_op jit(solution)/shard_map/all_gather | solution.py:96
  61.8 2.8 copy.31
  66.1 42.5 %while.88 = (s32[]{:T(128)}, f32[128]{0:T(128)S(1)}, f32[128]{0:T(128)S(1)}, f32[8,31,2048]{2,0,1:T(8,128)}, f32[128]{0:T(128)S(1)}, /*index=5*/f32[30,128]{1,0:T(8,128)S(1)}, s32[]{:T(128)}, s32[]{:T(128)}, s32[]{}) while((s32[]{:T(128)}, f32[128]{0:T(128)S(1)}, f32[128]{0:T(128)S(1)}, f32[8,31,2048]{2,0,1:T(8,128)}, ...), condition=%wide.region_5.6_spmd.clone, body=%wide.region_1.5_spmd.clone.sunk | while | flops 96330496 | bytes 3158143 | solution.py:55
  68.9 2.3 fusion.49
  74.2 2.3 fusion.49
  84.8 2.3 fusion.49
  90.1 2.3 fusion.49
  110.5 16.6 %while.84 = (s32[]{:T(128)}, f32[8,2048]{1,0:T(8,128)S(1)}, f32[8,2048]{1,0:T(8,128)S(1)}, f32[128]{0:T(128)S(1)}, f32[128]{0:T(128)S(1)}, /*index=5*/f32[8,30,2...) while((s32[]{:T(128)}, f32[8,2048]{1,0:T(8,128)S(1)}, f32[8,2048]{1,0:T(8,128)S(1)}, ...), condition=%wide.region_10.11_spmd, body=%wide.region_6.10_spmd.sunk | while | flops 96325632 | bytes 3186793 | solution.py:80
  127.8 5.8 %all-to-all-start = ((f32[32,1,512]{2,1,0:T(1,128)}), f32[32,1,512]{2,1,0:T(1,128)S(1)}, u32[]{:S(2)}, u32[]{:S(2)}) async-start(f32[32,1,512]{2,1,0:T(1,128)} %all_to_all.32), calls=%async_computation | async-start | bytes 131072 | tf_op jit(solution)/shard_map/all_to_all | solution.py:104
  134.4 5.6 %all-to-all-done = f32[32,1,512]{2,1,0:T(1,128)S(1)} async-done(((f32[32,1,512]{2,1,0:T(1,128)}), f32[32,1,512]{2,1,0:T(1,128)S(1)}, u32[]{:S(2)}, u32[]{:S(2)}) %all-to-all-start) | async-done | bytes 65568 | tf_op jit(solution)/shard_map/all_to_all | solution.py:104
  140.0 4.9 %all-to-all-start.1 = ((f32[32,1,512]{2,1,0:T(1,128)}), f32[32,1,512]{2,1,0:T(1,128)S(1)}, u32[]{:S(2)}, u32[]{:S(2)}) async-start(f32[32,1,512]{2,1,0:T(1,128)} %all_to_all.34), calls=%async_computation.1 | async-start | bytes 131072 | tf_op jit(solution)/shard_map/all_to_all | solution.py:111
  145.0 6.3 %all-to-all-done.1 = f32[32,1,512]{2,1,0:T(1,128)S(1)} async-done(((f32[32,1,512]{2,1,0:T(1,128)}), f32[32,1,512]{2,1,0:T(1,128)S(1)}, u32[]{:S(2)}, u32[]{:S(2)}) %all-to-all-start.1) | async-done | bytes 65568 | tf_op jit(solution)/shard_map/all_to_all | solution.py:111
  151.3 24.1 %all-gather.5 = f32[8,1,512]{2,1,0:T(1,128)S(1)} all-gather(f32[1,1,512]{2,1,0:T(1,128)S(1)} %bitcast.214), channel_id=3, replica_groups=mesh['row'=8,'col'=32] {'row'}, dimensions={0}, use_global_device_ids=true | all-gather | bytes 18432 | tf_op jit(solution)/shard_map/all_gather | solution.py:14
  175.4 21.5 %all-gather.4 = f32[8,1,512]{2,1,0:T(1,128)S(1)} all-gather(f32[1,1,512]{2,1,0:T(1,128)S(1)} %bitcast.213), channel_id=2, replica_groups=mesh['row'=8,'col'=32] {'row'}, dimensions={0}, use_global_device_ids=true | all-gather | bytes 18432 | tf_op jit(solution)/shard_map/all_gather | solution.py:14
  198.0 44.3 %all-gather.13.cloned.1.call-done = f32[31,16384]{1,0:T(8,128)} async-done(((f32[31,512]{1,0:T(8,128)}), f32[31,16384]{1,0:T(8,128)}) %all-gather.13.cloned.1.call-update) | async-done | bytes 2031632 | tf_op jit(solution)/shard_map/all_gather | solution.py:96
  242.3 2.8 copy.33
  246.6 42.5 %while.89 = (s32[]{:T(128)}, f32[128]{0:T(128)S(1)}, f32[128]{0:T(128)S(1)}, f32[8,31,2048]{2,0,1:T(8,128)}, f32[128]{0:T(128)S(1)}, /*index=5*/f32[30,128]{1,0:T(8,128)S(1)}, s32[]{:T(128)}, s32[]{:T(128)}, s32[]{}) while((s32[]{:T(128)}, f32[128]{0:T(128)S(1)}, f32[128]{0:T(128)S(1)}, f32[8,31,2048]{2,0,1:T(8,128)}, ...), condition=%wide.region_19.20_spmd.clone, body=%wide.region_15.0_spmd.clone.sunk | while | flops 96330496 | bytes 3158143 | solution.py:55
  291.1 16.6 %while.86 = (s32[]{:T(128)}, f32[8,2048]{1,0:T(8,128)S(1)}, f32[8,2048]{1,0:T(8,128)S(1)}, f32[128]{0:T(128)S(1)}, f32[128]{0:T(128)S(1)}, /*index=5*/f32[8,30,2...) while((s32[]{:T(128)}, f32[8,2048]{1,0:T(8,128)S(1)}, f32[8,2048]{1,0:T(8,128)S(1)}, ...), condition=%wide.region_24.25_spmd, body=%wide.region_20.24_spmd.sunk | while | flops 96325632 | bytes 3186793 | solution.py:80
  308.4 5.8 %all-to-all-start.2 = ((f32[32,1,512]{2,1,0:T(1,128)}), f32[32,1,512]{2,1,0:T(1,128)S(1)}, u32[]{:S(2)}, u32[]{:S(2)}) async-start(f32[32,1,512]{2,1,0:T(1,128)} %all_to_all.38), calls=%async_computation.2 | async-start | bytes 131072 | tf_op jit(solution)/shard_map/all_to_all | solution.py:104
  314.9 5.6 %all-to-all-done.2 = f32[32,1,512]{2,1,0:T(1,128)S(1)} async-done(((f32[32,1,512]{2,1,0:T(1,128)}), f32[32,1,512]{2,1,0:T(1,128)S(1)}, u32[]{:S(2)}, u32[]{:S(2)}) %all-to-all-start.2) | async-done | bytes 65568 | tf_op jit(solution)/shard_map/all_to_all | solution.py:104
  320.5 4.9 %all-to-all-start.3 = ((f32[32,1,512]{2,1,0:T(1,128)}), f32[32,1,512]{2,1,0:T(1,128)S(1)}, u32[]{:S(2)}, u32[]{:S(2)}) async-start(f32[32,1,512]{2,1,0:T(1,128)} %all_to_all.40), calls=%async_computation.3 | async-start | bytes 131072 | tf_op jit(solution)/shard_map/all_to_all | solution.py:111
  325.5 6.3 %all-to-all-done.3 = f32[32,1,512]{2,1,0:T(1,128)S(1)} async-done(((f32[32,1,512]{2,1,0:T(1,128)}), f32[32,1,512]{2,1,0:T(1,128)S(1)}, u32[]{:S(2)}, u32[]{:S(2)}) %all-to-all-start.3) | async-done | bytes 65568 | tf_op jit(solution)/shard_map/all_to_all | solution.py:111
  331.8 24.1 %all-gather.7 = f32[8,1,512]{2,1,0:T(1,128)S(1)} all-gather(f32[1,1,512]{2,1,0:T(1,128)S(1)} %bitcast.215), channel_id=5, replica_groups=mesh['row'=8,'col'=32] {'row'}, dimensions={0}, use_global_device_ids=true | all-gather | bytes 18432 | tf_op jit(solution)/shard_map/all_gather | solution.py:14
  356.0 21.3 %all-gather.6 = f32[8,1,512]{2,1,0:T(1,128)S(1)} all-gather(f32[1,1,512]{2,1,0:T(1,128)S(1)} %bitcast.212), channel_id=4, replica_groups=mesh['row'=8,'col'=32] {'row'}, dimensions={0}, use_global_device_ids=true | all-gather | bytes 18432 | tf_op jit(solution)/shard_map/all_gather | solution.py:14
  (305 shorter events, 122.7 us)
Async XLA Ops:
  7.2 54.7 %all-gather.11.cloned.1.call-start = ((), (), s32[]{:S(2)}) async-start(), calls=%async_computation.4 | async-start | bytes 2162688 | tf_op jit(solution)/shard_map/all_gather | solution.py:96
  64.6 1.4 copy-start.3
  66.1 42.5 %copy-start = (f32[31,16384]{1,0:T(8,128)S(1)}, f32[31,16384]{1,0:T(8,128)}, u32[]{:S(2)}) copy-start(f32[31,16384]{1,0:T(8,128)} %all-gather.11.cloned.1.call-done) | copy-start | bytes 6094852
  109.8 0.7 copy-start.5
  110.5 86.8 %copy-start.4 = (f32[512]{0:T(512)S(1)}, f32[512]{0:T(512)}, u32[]{:S(2)}) copy-start(f32[512]{0:T(512)} %param.20) | copy-start | bytes 6148
  110.5 86.8 %copy-start.2 = (f32[30,512]{1,0:T(8,128)S(1)}, f32[30,512]{1,0:T(8,128)}, u32[]{:S(2)}) copy-start(f32[30,512]{1,0:T(8,128)} %param.19) | copy-start | bytes 184324
  127.8 12.1 %all-to-all-start = ((f32[32,1,512]{2,1,0:T(1,128)}), f32[32,1,512]{2,1,0:T(1,128)S(1)}, u32[]{:S(2)}, u32[]{:S(2)}) async-start(f32[32,1,512]{2,1,0:T(1,128)} %all_to_all.32), calls=%async_computation | async-start | bytes 131072 | tf_op jit(solution)/shard_map/all_to_all | solution.py:104
  140.0 11.3 %all-to-all-start.1 = ((f32[32,1,512]{2,1,0:T(1,128)}), f32[32,1,512]{2,1,0:T(1,128)S(1)}, u32[]{:S(2)}, u32[]{:S(2)}) async-start(f32[32,1,512]{2,1,0:T(1,128)} %all_to_all.34), calls=%async_computation.1 | async-start | bytes 131072 | tf_op jit(solution)/shard_map/all_to_all | solution.py:111
  144.9 97.5 %all-gather.13.cloned.1.call-start = ((), (), s32[]{:S(2)}) async-start(), calls=%async_computation.5 | async-start | bytes 2162688 | tf_op jit(solution)/shard_map/all_gather | solution.py:96
  246.6 42.5 %copy-start.1 = (f32[31,16384]{1,0:T(8,128)S(1)}, f32[31,16384]{1,0:T(8,128)}, u32[]{:S(2)}) copy-start(f32[31,16384]{1,0:T(8,128)} %all-gather.13.cloned.1.call-done) | copy-start | bytes 6094852
  308.4 12.1 %all-to-all-start.2 = ((f32[32,1,512]{2,1,0:T(1,128)}), f32[32,1,512]{2,1,0:T(1,128)S(1)}, u32[]{:S(2)}, u32[]{:S(2)}) async-start(f32[32,1,512]{2,1,0:T(1,128)} %all_to_all.38), calls=%async_computation.2 | async-start | bytes 131072 | tf_op jit(solution)/shard_map/all_to_all | solution.py:104
  320.5 11.3 %all-to-all-start.3 = ((f32[32,1,512]{2,1,0:T(1,128)}), f32[32,1,512]{2,1,0:T(1,128)S(1)}, u32[]{:S(2)}, u32[]{:S(2)}) async-start(f32[32,1,512]{2,1,0:T(1,128)} %all_to_all.40), calls=%async_computation.3 | async-start | bytes 131072 | tf_op jit(solution)/shard_map/all_to_all | solution.py:111
Sparse Core Ops, SparseCore 0:
  10.6 51.2 all-gather.10
  198.1 44.1 all-gather.12
where the time goes:
time: 387 us; the launch traced here: 385 us
  waiting for transfers between devices  120 us (31%)
  blocking collectives  91 us (24%)
  local copies, waits for them, and re-layouts  65.8 us (17%)
  matrix products  54.9 us (14%)
  starting transfers between devices  21.6 us (6%)
  other arithmetic  15.7 us (4%)
  between operations  14.3 us (4%)
    all_gather x2, waiting for transfers between devices, on_device(): gathered = lax.all_gather(target_pack, 'col', axis=1, tiled=True)  96 us
    all_gather x4, blocking collectives, merged(): everything = jax.tree.map(lambda part: lax.all_gather(part, axis), shard)  91 us
    dot_general x16, matrix products, tile_scores(): lax.dot_general(own_coords, coords, (((0,), (0,)), ((), ())), precision=l...  36.3 us
    slice x16, local copies, waits for them, and re-layouts, tile_scores(): coords = other[:dims]  28 us
    dot_general x16, matrix products, one_block(): lax.dot_general(row_block[:dims], block, (((0,), (0,)), ((), ())), precis...  18.6 us
    slice x16, local copies, waits for them, and re-layouts, tile_scores(): return other[dims][None, :] - cost / entropic_scale  13.7 us
    all_to_all x2, waiting for transfers between devices, on_device(): lax.all_to_all(wide_total.reshape(blocks_count, own_cols), 'col', split_a...  12.6 us
    all_to_all x2, starting transfers between devices, on_device(): lax.all_to_all(wide_peak.reshape(blocks_count, own_cols), 'col', split_ax...  11.7 us
  transfers between devices with their start and end apart: 6, of which 6 were waited for; matrix products, arithmetic and copies ran while one was open for 0% of the time, Pallas kernels for 0%

commit v1 on v0

--- a/solution.py
+++ b/solution.py
@@ -1,3 +1,4 @@
+import functools
 import math
 import jax
 import jax.numpy as jnp
@@ -8,6 +9,19 @@
 entropic_scale = 2.0
 lowest = -1e30
 block_width = 2048
+
+
+def refer_sections_on_mesh(v0, dim_i):
+    copies = []
+    for _ in range(jax.lax.psum(1, axis_name="col")):
+        copies.append(v0)
+    return jnp.concatenate(
+        jax.lax.all_to_all(jnp.stack(copies, axis=0), "col", split_axis=0, concat_axis=0),
+        axis=dim_i,
+    )
+
+
+get_cubes_now = functools.partial(refer_sections_on_mesh, dim_i=1)
 
 
 def merged(shard, axis, combine):
@@ -93,7 +107,7 @@
             jnp.full((own_rows,), lowest, jnp.float32),
             jnp.zeros((own_rows,), jnp.float32),
         )
-        gathered = lax.all_gather(target_pack, "col", axis=1, tiled=True)
+        gathered = get_cubes_now(target_pack)
         row_peak, row_total = online_fold(sources, row_start, gathered)
         row_potential = -entropic_scale * (row_peak + jnp.log(row_total))
         source_term = row_potential / entropic_scale + log_source_mass

time: 387 us -> 355 us (0.917)
  waiting for transfers between devices: 120 us -> 79.9 us
  between operations: 14.3 us -> 0.88 us
  starting transfers between devices: 21.6 us -> 34.5 us
  local copies, waits for them, and re-layouts: 65.8 us -> 77.5 us
    all_gather x2 -> x0, waiting for transfers between devices: 96 us -> none  [on_device(): gathered = lax.all_gather(target_pack, 'col', axis=1, tiled=True)]
    all_to_all x0 -> x2, waiting for transfers between devices: none -> 55.9 us  [refer_sections_on_mesh(): jax.lax.all_to_all(jnp.stack(copies, axis=0), 'col', split_axis=0, concat...]
    all_to_all x0 -> x2, starting transfers between devices: none -> 12.9 us  [refer_sections_on_mesh(): jax.lax.all_to_all(jnp.stack(copies, axis=0), 'col', split_axis=0, concat...]
    another operation x4 -> x8, local copies, waits for them, and re-layouts: 0.02 us -> 9.59 us  [the longest x2 6.34 us: online_fold(): piece.reshape(piece.shape[0], length // width, width).transpose(1, 0, 2)]
    reshape x0 -> x4, local copies, waits for them, and re-layouts: none -> 9.24 us  [the longest x2 4.92 us: refer_sections_on_mesh(): jnp.concatenate(jax.lax.all_to_all(jnp.stack(copies, axis=0), 'col', spli...]
    unnamed x20 -> x12, local copies, waits for them, and re-layouts: 8.54 us -> 0.03 us
    slice x0 -> x2, local copies, waits for them, and re-layouts: none -> 4.85 us  [column_partials(): coords = all_columns[:dims]]
where the time goes in v1:
time: 355 us; the launch traced here: 353 us
  blocking collectives  89.7 us (25%)
  waiting for transfers between devices  79.9 us (23%)
  local copies, waits for them, and re-layouts  77.5 us (22%)
  matrix products  54.9 us (15%)
  starting transfers between devices  34.5 us (10%)
  other arithmetic  13.8 us (4%)
    all_gather x4, blocking collectives, merged(): everything = jax.tree.map(lambda part: lax.all_gather(part, axis), shard)  89.7 us
    all_to_all x2, waiting for transfers between devices, refer_sections_on_mesh(): jax.lax.all_to_all(jnp.stack(copies, axis=0), 'col', split_axis=0, concat...  55.9 us
    dot_general x16, matrix products, tile_scores(): lax.dot_general(own_coords, coords, (((0,), (0,)), ((), ())), precision=l...  36.3 us
    slice x16, local copies, waits for them, and re-layouts, tile_scores(): coords = other[:dims]  27.7 us
    dot_general x16, matrix products, one_block(): lax.dot_general(row_block[:dims], block, (((0,), (0,)), ((), ())), precis...  18.6 us
    slice x16, local copies, waits for them, and re-layouts, tile_scores(): return other[dims][None, :] - cost / entropic_scale  13.7 us
    all_to_all x2, starting transfers between devices, refer_sections_on_mesh(): jax.lax.all_to_all(jnp.stack(copies, axis=0), 'col', split_axis=0, concat...  12.9 us
    all_to_all x2, waiting for transfers between devices, on_device(): lax.all_to_all(wide_total.reshape(blocks_count, own_cols), 'col', split_a...  12.7 us
  transfers between devices with their start and end apart: 6, of which 6 were waited for; matrix products, arithmetic and copies ran while one was open for 0% of the time, Pallas kernels for 0%

profile of v1, /device:TPU:2, one launch (start us, length us, event | category | flops | bytes accessed | tf_op | source)
XLA Modules:
  0.0 353.0 jit_solution(15741075475678332288)
XLA Ops:
  3.8 7.8 %all-to-all-start = ((f32[32,31,512]{2,1,0:T(8,128)}), f32[32,31,512]{2,1,0:T(8,128)S(1)}, u32[]{:S(2)}, u32[]{:S(2)}) async-start(f32[32,31,512]{2,1,0:T(8,128)} %stack.4), calls=%async_computation | async-start | bytes 4194304 | tf_op jit(solution)/shard_map/all_to_all | solution.py:19
  11.6 27.9 %all-to-all-done = f32[32,31,512]{2,1,0:T(8,128)S(1)} async-done(((f32[32,31,512]{2,1,0:T(8,128)}), f32[32,31,512]{2,1,0:T(8,128)S(1)}, u32[]{:S(2)}, u32[]{:S(2)}) %all-to-all-start) | async-done | bytes 2031648 | tf_op jit(solution)/shard_map/all_to_all | solution.py:19
  39.5 2.5 copy.11
  41.9 3.2 reshape_reshape.4
  45.1 42.4 %while.88 = (s32[]{:T(128)}, f32[128]{0:T(128)S(1)}, f32[128]{0:T(128)S(1)}, f32[8,31,2048]{2,0,1:T(8,128)}, f32[128]{0:T(128)S(1)}, /*index=5*/f32[30,128]{1,0:T(8,128)S(1)}, s32[]{:T(128)}, s32[]{:T(128)}, s32[]{}) while((s32[]{:T(128)}, f32[128]{0:T(128)S(1)}, f32[128]{0:T(128)S(1)}, f32[8,31,2048]{2,0,1:T(8,128)}, ...), condition=%wide.region_5.6_spmd.clone, body=%wide.region_1.5_spmd.clone.sunk | while | flops 96330496 | bytes 3158143 | solution.py:69
  92.2 16.6 %while.84 = (s32[]{:T(128)}, f32[8,2048]{1,0:T(8,128)S(1)}, f32[8,2048]{1,0:T(8,128)S(1)}, f32[128]{0:T(128)S(1)}, f32[128]{0:T(128)S(1)}, /*index=5*/f32[8,30,2...) while((s32[]{:T(128)}, f32[8,2048]{1,0:T(8,128)S(1)}, f32[8,2048]{1,0:T(8,128)S(1)}, ...), condition=%wide.region_10.11_spmd, body=%wide.region_6.10_spmd.sunk | while | flops 96325632 | bytes 3186793 | solution.py:94
  109.5 5.9 %all-to-all-start.1 = ((f32[32,1,512]{2,1,0:T(1,128)}), f32[32,1,512]{2,1,0:T(1,128)S(1)}, u32[]{:S(2)}, u32[]{:S(2)}) async-start(f32[32,1,512]{2,1,0:T(1,128)} %all_to_all.39), calls=%async_computation.1 | async-start | bytes 131072 | tf_op jit(solution)/shard_map/all_to_all | solution.py:118
  116.1 5.7 %all-to-all-done.1 = f32[32,1,512]{2,1,0:T(1,128)S(1)} async-done(((f32[32,1,512]{2,1,0:T(1,128)}), f32[32,1,512]{2,1,0:T(1,128)S(1)}, u32[]{:S(2)}, u32[]{:S(2)}) %all-to-all-start.1) | async-done | bytes 65568 | tf_op jit(solution)/shard_map/all_to_all | solution.py:118
  121.7 4.9 %all-to-all-start.2 = ((f32[32,1,512]{2,1,0:T(1,128)}), f32[32,1,512]{2,1,0:T(1,128)S(1)}, u32[]{:S(2)}, u32[]{:S(2)}) async-start(f32[32,1,512]{2,1,0:T(1,128)} %all_to_all.41), calls=%async_computation.2 | async-start | bytes 131072 | tf_op jit(solution)/shard_map/all_to_all | solution.py:125
  126.7 6.3 %all-to-all-done.2 = f32[32,1,512]{2,1,0:T(1,128)S(1)} async-done(((f32[32,1,512]{2,1,0:T(1,128)}), f32[32,1,512]{2,1,0:T(1,128)S(1)}, u32[]{:S(2)}, u32[]{:S(2)}) %all-to-all-start.2) | async-done | bytes 65568 | tf_op jit(solution)/shard_map/all_to_all | solution.py:125
  133.1 25.6 %all-gather.5 = f32[8,1,512]{2,1,0:T(1,128)S(1)} all-gather(f32[1,1,512]{2,1,0:T(1,128)S(1)} %bitcast.200), channel_id=3, replica_groups=mesh['row'=8,'col'=32] {'row'}, dimensions={0}, use_global_device_ids=true | all-gather | bytes 18432 | tf_op jit(solution)/shard_map/all_gather | solution.py:28
  158.7 21.3 %all-gather.4 = f32[8,1,512]{2,1,0:T(1,128)S(1)} all-gather(f32[1,1,512]{2,1,0:T(1,128)S(1)} %bitcast.199), channel_id=2, replica_groups=mesh['row'=8,'col'=32] {'row'}, dimensions={0}, use_global_device_ids=true | all-gather | bytes 18432 | tf_op jit(solution)/shard_map/all_gather | solution.py:28
  182.0 5.1 %all-to-all-start.3 = ((f32[32,31,512]{2,1,0:T(8,128)}), f32[32,31,512]{2,1,0:T(8,128)S(1)}, u32[]{:S(2)}, u32[]{:S(2)}) async-start(f32[32,31,512]{2,1,0:T(8,128)} %stack.5), calls=%async_computation.3 | async-start | bytes 4194304 | tf_op jit(solution)/shard_map/all_to_all | solution.py:19
  187.2 28.0 %all-to-all-done.3 = f32[32,31,512]{2,1,0:T(8,128)S(1)} async-done(((f32[32,31,512]{2,1,0:T(8,128)}), f32[32,31,512]{2,1,0:T(8,128)S(1)}, u32[]{:S(2)}, u32[]{:S(2)}) %all-to-all-start.3) | async-done | bytes 2031648 | tf_op jit(solution)/shard_map/all_to_all | solution.py:19
  215.2 2.5 copy.15
  217.6 3.2 reshape_reshape.5
  220.8 42.4 %while.89 = (s32[]{:T(128)}, f32[128]{0:T(128)S(1)}, f32[128]{0:T(128)S(1)}, f32[8,31,2048]{2,0,1:T(8,128)}, f32[128]{0:T(128)S(1)}, /*index=5*/f32[30,128]{1,0:T(8,128)S(1)}, s32[]{:T(128)}, s32[]{:T(128)}, s32[]{}) while((s32[]{:T(128)}, f32[128]{0:T(128)S(1)}, f32[128]{0:T(128)S(1)}, f32[8,31,2048]{2,0,1:T(8,128)}, ...), condition=%wide.region_19.20_spmd.clone, body=%wide.region_15.0_spmd.clone.sunk | while | flops 96330496 | bytes 3158143 | solution.py:69
  268.3 16.6 %while.86 = (s32[]{:T(128)}, f32[8,2048]{1,0:T(8,128)S(1)}, f32[8,2048]{1,0:T(8,128)S(1)}, f32[128]{0:T(128)S(1)}, f32[128]{0:T(128)S(1)}, /*index=5*/f32[8,30,2...) while((s32[]{:T(128)}, f32[8,2048]{1,0:T(8,128)S(1)}, f32[8,2048]{1,0:T(8,128)S(1)}, ...), condition=%wide.region_24.25_spmd, body=%wide.region_20.24_spmd.sunk | while | flops 96325632 | bytes 3186793 | solution.py:94
  285.6 5.9 %all-to-all-start.4 = ((f32[32,1,512]{2,1,0:T(1,128)}), f32[32,1,512]{2,1,0:T(1,128)S(1)}, u32[]{:S(2)}, u32[]{:S(2)}) async-start(f32[32,1,512]{2,1,0:T(1,128)} %all_to_all.46), calls=%async_computation.4 | async-start | bytes 131072 | tf_op jit(solution)/shard_map/all_to_all | solution.py:118
  292.2 5.7 %all-to-all-done.4 = f32[32,1,512]{2,1,0:T(1,128)S(1)} async-done(((f32[32,1,512]{2,1,0:T(1,128)}), f32[32,1,512]{2,1,0:T(1,128)S(1)}, u32[]{:S(2)}, u32[]{:S(2)}) %all-to-all-start.4) | async-done | bytes 65568 | tf_op jit(solution)/shard_map/all_to_all | solution.py:118
  297.9 4.9 %all-to-all-start.5 = ((f32[32,1,512]{2,1,0:T(1,128)}), f32[32,1,512]{2,1,0:T(1,128)S(1)}, u32[]{:S(2)}, u32[]{:S(2)}) async-start(f32[32,1,512]{2,1,0:T(1,128)} %all_to_all.48), calls=%async_computation.5 | async-start | bytes 131072 | tf_op jit(solution)/shard_map/all_to_all | solution.py:125
  302.9 6.3 %all-to-all-done.5 = f32[32,1,512]{2,1,0:T(1,128)S(1)} async-done(((f32[32,1,512]{2,1,0:T(1,128)}), f32[32,1,512]{2,1,0:T(1,128)S(1)}, u32[]{:S(2)}, u32[]{:S(2)}) %all-to-all-start.5) | async-done | bytes 65568 | tf_op jit(solution)/shard_map/all_to_all | solution.py:125
  309.3 21.4 %all-gather.7 = f32[8,1,512]{2,1,0:T(1,128)S(1)} all-gather(f32[1,1,512]{2,1,0:T(1,128)S(1)} %bitcast.201), channel_id=5, replica_groups=mesh['row'=8,'col'=32] {'row'}, dimensions={0}, use_global_device_ids=true | all-gather | bytes 18432 | tf_op jit(solution)/shard_map/all_gather | solution.py:28
  330.7 21.4 %all-gather.6 = f32[8,1,512]{2,1,0:T(1,128)S(1)} all-gather(f32[1,1,512]{2,1,0:T(1,128)S(1)} %bitcast.198), channel_id=4, replica_groups=mesh['row'=8,'col'=32] {'row'}, dimensions={0}, use_global_device_ids=true | all-gather | bytes 18432 | tf_op jit(solution)/shard_map/all_gather | solution.py:28
  (301 shorter events, 135.7 us)
Async XLA Ops:
  3.8 7.8 %copy-start.1 = (f32[30,128]{1,0:T(8,128)S(1)}, f32[30,128]{1,0:T(8,128)}, u32[]{:S(2)}) copy-start(f32[30,128]{1,0:T(8,128)} %param.17) | copy-start | bytes 46084
  3.8 35.7 %all-to-all-start = ((f32[32,31,512]{2,1,0:T(8,128)}), f32[32,31,512]{2,1,0:T(8,128)S(1)}, u32[]{:S(2)}, u32[]{:S(2)}) async-start(f32[32,31,512]{2,1,0:T(8,128)} %stack.4), calls=%async_computation | async-start | bytes 4194304 | tf_op jit(solution)/shard_map/all_to_all | solution.py:19
  89.9 2.2 copy-start.3
  92.2 88.2 %copy-start.2 = (f32[512]{0:T(512)S(1)}, f32[512]{0:T(512)}, u32[]{:S(2)}) copy-start(f32[512]{0:T(512)} %param.20) | copy-start | bytes 6148
  92.2 88.2 %copy-start = (f32[30,512]{1,0:T(8,128)S(1)}, f32[30,512]{1,0:T(8,128)}, u32[]{:S(2)}) copy-start(f32[30,512]{1,0:T(8,128)} %param.19) | copy-start | bytes 184324
  109.5 12.3 %all-to-all-start.1 = ((f32[32,1,512]{2,1,0:T(1,128)}), f32[32,1,512]{2,1,0:T(1,128)S(1)}, u32[]{:S(2)}, u32[]{:S(2)}) async-start(f32[32,1,512]{2,1,0:T(1,128)} %all_to_all.39), calls=%async_computation.1 | async-start | bytes 131072 | tf_op jit(solution)/shard_map/all_to_all | solution.py:118
  121.7 11.3 %all-to-all-start.2 = ((f32[32,1,512]{2,1,0:T(1,128)}), f32[32,1,512]{2,1,0:T(1,128)S(1)}, u32[]{:S(2)}, u32[]{:S(2)}) async-start(f32[32,1,512]{2,1,0:T(1,128)} %all_to_all.41), calls=%async_computation.2 | async-start | bytes 131072 | tf_op jit(solution)/shard_map/all_to_all | solution.py:125
  182.0 33.1 %all-to-all-start.3 = ((f32[32,31,512]{2,1,0:T(8,128)}), f32[32,31,512]{2,1,0:T(8,128)S(1)}, u32[]{:S(2)}, u32[]{:S(2)}) async-start(f32[32,31,512]{2,1,0:T(8,128)} %stack.5), calls=%async_computation.3 | async-start | bytes 4194304 | tf_op jit(solution)/shard_map/all_to_all | solution.py:19
  285.6 12.3 %all-to-all-start.4 = ((f32[32,1,512]{2,1,0:T(1,128)}), f32[32,1,512]{2,1,0:T(1,128)S(1)}, u32[]{:S(2)}, u32[]{:S(2)}) async-start(f32[32,1,512]{2,1,0:T(1,128)} %all_to_all.46), calls=%async_computation.4 | async-start | bytes 131072 | tf_op jit(solution)/shard_map/all_to_all | solution.py:118
  297.9 11.3 %all-to-all-start.5 = ((f32[32,1,512]{2,1,0:T(1,128)}), f32[32,1,512]{2,1,0:T(1,128)S(1)}, u32[]{:S(2)}, u32[]{:S(2)}) async-start(f32[32,1,512]{2,1,0:T(1,128)} %all_to_all.48), calls=%async_computation.5 | async-start | bytes 131072 | tf_op jit(solution)/shard_map/all_to_all | solution.py:125
